TPU v7x, 32 devices: a whole 2x2x4 slice. The times are simulated.
32 devices in a mesh: expert: 8 (over z, x), replica: 4 (over y, core).
Axes of the slice: x: 2, y: 2, z: 4, core: 2. Of those that a mesh axis runs over, the one named last changes fastest.
Arguments:
- tokens: bfloat16 [4096, 2048], P(('expert', 'replica')), may hold values from -6 to 6
- cotangent: bfloat16 [4096, 2048], P(('expert', 'replica')), may hold values from -6 to 6
- route_weights: float32 [4096, 8], P(('expert', 'replica')), may hold values from 0.02 to 0.4
- expert_ids: int32 [4096, 8], P(('expert', 'replica')), may hold values from 0 to 15, as said below
- slot_ids: int32 [4096, 8], P(('expert', 'replica')), may hold values from 0 to 63, as said below
- kept_mask: int32 [4096, 8], P(('expert', 'replica')), may hold values from 0 to 1, as said below
- gate_weight: bfloat16 [16, 2048, 384], P('expert'), may hold values from -0.125 to 0.125
- up_weight: bfloat16 [16, 2048, 384], P('expert'), may hold values from -0.125 to 0.125
- down_weight: bfloat16 [16, 384, 2048], P('expert'), may hold values from -0.3125 to 0.3125
- projector_basis: float32 [2048, 256], P('expert'), may hold values from -6 to 6
Outputs:
- token_grads: bfloat16 [4096, 2048], P(('expert', 'replica'))
- projected_grads: float32 [16, 3, 384, 256], P('expert')
- new_basis: float32 [2048, 256], P('expert')
Inputs may be any that keep to these rules, and one draw needn't show every extreme that they name: `expert_ids`: each row names 8 different experts. `slot_ids`: within one device's rows, the kept routes to one expert take slots 0, 1, 2, ... in the order of rows and then of the position in the row; a dropped route has slot 0; in every draw some expert receives 64 kept routes from every device's rows. `kept_mask`: a route is dropped exactly when 64 earlier routes of the same device's rows go to the same expert.
All inputs are finite; a program needn't handle non-finite values.
Results may differ from a plain program's by a relative error of at most 0.019.
Values may be sent and summed in bfloat16 or wider, within the bound.
A program may use at most 128 MiB of HBM per device.

v0:
```python
import math
import jax
import jax.numpy as jnp
from jax import lax
from jax.sharding import PartitionSpec as P


def body(
    tokens,
    cotangent,
    route_weights,
    expert_ids,
    slot_ids,
    kept_mask,
    gate_weight,
    up_weight,
    down_weight,
    projector_basis,
):
    tok_count, model_width = tokens.shape
    route_top = expert_ids.shape[1]
    local_count = gate_weight.shape[0]
    group_count = lax.axis_size("expert")
    expert_total = local_count * group_count
    slot_cap = tok_count * route_top // expert_total
    slot_total = expert_total * slot_cap
    route_count = tok_count * route_top
    target = jnp.where(kept_mask > 0, expert_ids * slot_cap + slot_ids, slot_total).reshape(-1)
    table = (
        jnp.full((slot_total,), route_count, jnp.int32)
        .at[target]
        .set(jnp.arange(route_count, dtype=jnp.int32), mode="drop")
    )
    owner = table // route_top
    tokens_pad = jnp.concatenate([tokens, jnp.zeros((1, model_width), tokens.dtype)], 0)
    cotangent_pad = jnp.concatenate([cotangent, jnp.zeros((1, model_width), cotangent.dtype)], 0)
    weight_pad = jnp.concatenate([route_weights.reshape(-1), jnp.zeros((1,), jnp.float32)], 0)
    x_send = tokens_pad[owner].reshape(group_count, local_count * slot_cap, model_width)
    dy_send = (cotangent_pad[owner].astype(jnp.float32) * weight_pad[table][:, None]).astype(
        jnp.bfloat16
    )
    dy_send = dy_send.reshape(group_count, local_count * slot_cap, model_width)
    full_basis = lax.all_gather(
        projector_basis.astype(jnp.bfloat16), "expert", axis=0, tiled=True
    ).astype(projector_basis.dtype)
    projector = (full_basis * (1.0 / math.sqrt(model_width))).astype(jnp.bfloat16)
    block_shape = (group_count, local_count, slot_cap, model_width)
    x_recv, dy_recv = (
        lax.all_to_all(x_send, "expert", split_axis=0, concat_axis=0, tiled=True),
        lax.all_to_all(dy_send, "expert", split_axis=0, concat_axis=0, tiled=True),
    )
    x_rows = x_recv.reshape(block_shape)
    gate = jnp.einsum("sjcd,jdf->sjcf", x_rows, gate_weight, preferred_element_type=jnp.float32)
    upper = jnp.einsum("sjcd,jdf->sjcf", x_rows, up_weight, preferred_element_type=jnp.float32)
    sigma = jax.nn.sigmoid(gate)
    activated = gate * sigma
    slope = sigma * (1.0 + gate * (1.0 - sigma))
    hidden = (activated * upper).astype(jnp.bfloat16)
    x_proj = jnp.einsum(
        "sjcd,dr->sjcr", x_rows, projector, preferred_element_type=jnp.float32
    ).astype(jnp.bfloat16)
    x_rows, upper, activated, slope, hidden, x_proj = (
        x_rows,
        upper,
        activated,
        slope,
        hidden,
        x_proj,
    )
    dy_rows = dy_recv.reshape(block_shape)
    hidden_grad = jnp.einsum(
        "sjcd,jfd->sjcf", dy_rows, down_weight, preferred_element_type=jnp.float32
    )
    up_grad = (hidden_grad * activated).astype(jnp.bfloat16)
    gate_grad = (hidden_grad * upper * slope).astype(jnp.bfloat16)
    row_grads = jnp.einsum(
        "sjcf,jdf->sjcd", gate_grad, gate_weight, preferred_element_type=jnp.float32
    )
    row_grads = row_grads + jnp.einsum(
        "sjcf,jdf->sjcd", up_grad, up_weight, preferred_element_type=jnp.float32
    )
    row_grads = row_grads.astype(jnp.bfloat16).reshape(
        group_count, local_count * slot_cap, model_width
    )
    returned = lax.all_to_all(row_grads, "expert", split_axis=0, concat_axis=0, tiled=True).reshape(
        slot_total, model_width
    )
    returned = jnp.concatenate([returned, jnp.zeros((1, model_width), jnp.bfloat16)], 0)
    token_grads = jnp.sum(
        returned[target].reshape(tok_count, route_top, model_width).astype(jnp.float32), axis=1
    ).astype(jnp.bfloat16)
    dy_proj = jnp.einsum(
        "sjcd,dr->sjcr", dy_rows, projector, preferred_element_type=jnp.float32
    ).astype(jnp.bfloat16)
    partial_grads = jnp.stack(
        [
            jnp.einsum("sjcf,sjcr->jfr", gate_grad, x_proj, preferred_element_type=jnp.float32),
            jnp.einsum("sjcf,sjcr->jfr", up_grad, x_proj, preferred_element_type=jnp.float32),
            jnp.einsum("sjcf,sjcr->jfr", hidden, dy_proj, preferred_element_type=jnp.float32),
        ],
        1,
    )
    projected_grads = lax.psum(partial_grads, "replica")
    grads_low = projected_grads.astype(jnp.bfloat16)
    mixed = jnp.einsum(
        "sjcf,jfr->sjcr", gate_grad, grads_low[:, 0], preferred_element_type=jnp.float32
    )
    mixed = (
        mixed
        + jnp.einsum("sjcf,jfr->sjcr", up_grad, grads_low[:, 1], preferred_element_type=jnp.float32)
    ).astype(jnp.bfloat16)
    down_mix = jnp.einsum(
        "sjcf,jfr->sjcr", hidden, grads_low[:, 2], preferred_element_type=jnp.float32
    ).astype(jnp.bfloat16)
    power = jnp.einsum("sjcd,sjcr->dr", x_rows, mixed, preferred_element_type=jnp.float32)
    power = power + jnp.einsum(
        "sjcd,sjcr->dr", dy_rows, down_mix, preferred_element_type=jnp.float32
    )
    panel_rows = model_width // group_count
    power_sum = lax.psum(power, ("expert", "replica"))
    gram_total = jnp.dot(
        power_sum.T, power_sum, precision=lax.Precision.HIGHEST, preferred_element_type=jnp.float32
    )
    own_panel = lax.dynamic_slice_in_dim(
        power_sum, lax.axis_index("expert") * panel_rows, panel_rows, 0
    )
    lower = jnp.linalg.cholesky(gram_total)
    new_basis = (
        math.sqrt(model_width) * jax.scipy.linalg.solve_triangular(lower, own_panel.T, lower=True).T
    )
    return (token_grads, projected_grads, new_basis)


def solution(mesh):
    return jax.shard_map(
        body,
        mesh=mesh,
        in_specs=(
            P(("expert", "replica"), None),
            P(("expert", "replica"), None),
            P(("expert", "replica"), None),
            P(("expert", "replica"), None),
            P(("expert", "replica"), None),
            P(("expert", "replica"), None),
            P("expert", None, None),
            P("expert", None, None),
            P("expert", None, None),
            P("expert", None),
        ),
        out_specs=(
            P(("expert", "replica"), None),
            P("expert", None, None, None),
            P("expert", None),
        ),
        check_vma=False,
    )
```

profile of v0, /device:TPU:0, one launch (start us, length us, event | category | flops | bytes accessed | tf_op | source)
XLA Modules:
  0.0 595.4 jit_solution(13270312014699253039)
XLA Ops:
  8.3 4.3 scatter_custom_fusion
  15.4 10.0 %gather_fusion = bf16[1024,2048]{1,0:T(8,128)(2,1)} fusion(bf16[129,2048]{1,0:T(8,128)(2,1)} %concatenate.15, s32[1024]{0:T(1024)S(1)} %get-tuple-element.37), kind=kCustom, calls=%fused_computation | custom fusion | bytes 8392704 | tf_op jit(solution)/shard_map/gather | solution.py:39
  25.4 6.1 %gather_fusion.1 = f32[1024]{0:T(1024)S(1)} fusion(f32[1025]{0:T(1024)S(1)} %pad_maximum_fusion.1, s32[1024]{0:T(1024)S(1)} %get-tuple-element.36), kind=kCustom, calls=%fused_computation.1 | custom fusion | bytes 12288 | tf_op jit(solution)/shard_map/gather | solution.py:39
  31.5 4.9 fusion
  36.4 7.3 %all-to-all-start = ((bf16[8,128,2048]{2,1,0:T(8,128)(2,1)}), bf16[8,128,2048]{2,1,0:T(8,128)(2,1)}, u32[]{:S(2)}, u32[]{:S(2)}) async-start(bf16[8,128,2048]{2,1,0:T(8,128)(2,1)} %fusion), calls=%async_computation | async-start | bytes 8388608 | tf_op jit(solution)/shard_map/all_to_all | solution.py:50
  45.6 10.0 %gather_fusion.2 = bf16[1024,2048]{1,0:T(8,128)(2,1)} fusion(bf16[129,2048]{1,0:T(8,128)(2,1)} %concatenate.17, s32[1024]{0:T(1024)S(1)} %get-tuple-element.37), kind=kCustom, calls=%fused_computation.2 | custom fusion | bytes 8392704 | tf_op jit(solution)/shard_map/gather | solution.py:38
  55.6 81.4 %all-to-all-done = bf16[8,128,2048]{2,1,0:T(8,128)(2,1)} async-done(((bf16[8,128,2048]{2,1,0:T(8,128)(2,1)}), bf16[8,128,2048]{2,1,0:T(8,128)(2,1)}, u32[]{:S(2)}, u32[]{:S(2)}) %all-to-all-start) | async-done | bytes 4194336 | tf_op jit(solution)/shard_map/all_to_all | solution.py:50
  137.0 4.7 all-to-all-start.1
  143.0 6.6 %fusion.12 = f32[2,8,64,384]{3,2,1,0:T(8,128)} fusion(bf16[8,2,64,2048]{3,2,1,0:T(8,128)(2,1)} %bitcast.3, bf16[2,384,2048]{2,1,0:T(8,128)(2,1)} %param.18), kind=kOutput, calls=%fused_computation.22 | convolution fusion | flops 1610612736 | bytes 8912896 | tf_op jit(solution)/shard_map/sjcd,jfd->sjcf/dot_general | solution.py:71
  149.6 97.3 %all-to-all-done.1 = bf16[8,128,2048]{2,1,0:T(8,128)(2,1)} async-done(((bf16[8,128,2048]{2,1,0:T(8,128)(2,1)}), bf16[8,128,2048]{2,1,0:T(8,128)(2,1)}, u32[]{:S(2)}, u32[]{:S(2)}) %all-to-all-start.1) | async-done | bytes 4194336 | tf_op jit(solution)/shard_map/all_to_all | solution.py:49
  246.9 5.6 fusion.4
  252.6 6.3 %fusion.36 = (bf16[8,2,64,384]{3,2,0,1:T(8,128)(2,1)}, bf16[8,2,64,384]{3,2,0,1:T(8,128)(2,1)S(1)}, bf16[8,2,64,384]{3,2,0,1:T(8,128)(2,1)}) fusion(f32[2,8,64,384]{3,2,1,0:T(8,128)S(1)} %fusion.4, f32[2,8,64,384]{3,2,1,0:T(8,128)S(1)} %copy-done.13, bf16[2,2048,384]{2,1,0:T(8,128)(2,1)S(1)} %copy-done, bf16[8,2,64,2048]{3,2,1,0:T(8,128)(2,1)} %bitcast.8), kind=kOutput, calls=%fused_computation.47 | convolution fusion | flops 1616510976 | bytes 12845056 | tf_op jit(solution)/shard_map/sjcd,jdf->sjcf/dot_general | solution.py:54
  259.8 5.6 fusion.14
  265.4 3.9 convolution_convert_fusion.1
  269.3 2.7 convolution_bitcast_fusion.2
  273.4 2.4 fusion.1
  275.8 2.5 copy.24
  278.3 4.7 all-to-all-start.2
  283.1 4.4 convolution_bitcast_fusion
  289.4 56.9 %all-reduce.7.cloned.1.call-done = f32[2,3,384,256]{3,2,0,1:T(8,128)} async-done(((f32[2,3,384,256]{3,2,0,1:T(8,128)}), f32[2,3,384,256]{3,2,0,1:T(8,128)}) %all-reduce.7.cloned.1.call-update) | async-done | bytes 2359312 | tf_op jit(solution)/shard_map/psum | solution.py:103
  349.6 5.4 fusion.20
  355.0 6.4 %fusion.26 = f32[2048,256]{1,0:T(8,128)} fusion(f32[2048,256]{1,0:T(8,128)} %fusion.20, bf16[8,2,64,2048]{3,2,1,0:T(8,128)(2,1)} %bitcast.8, f32[2,256,8,64]{1,3,2,0:T(8,128)} %fusion.52, bf16[8,2,64,384]{3,2,0,1:T(8,128)(2,1)S(1)} %copy-done.9, bf16[2,3,384,256]{3,2,0,1:T(8,128)(2,1)} %copy-done.7), kind=kOutput, calls=%fused_computation.32 | convolution fusion | flops 1276116992 | bytes 10616832 | tf_op jit(solution)/shard_map/sjcd,sjcr->dr/dot_general | solution.py:115
  363.2 134.4 %all-reduce.9.cloned.1.call-done = f32[2048,256]{1,0:T(8,128)} async-done(((f32[2048,256]{1,0:T(8,128)}), f32[2048,256]{1,0:T(8,128)}) %all-reduce.9.cloned.1.call-update) | async-done | bytes 2097168 | tf_op jit(solution)/shard_map/psum | solution.py:120
  497.6 5.7 fusion.72
  503.5 11.7 %cholesky.50 = f32[128,128]{1,0:T(8,128)S(1)} custom-call(f32[128,128]{1,0:T(8,128)S(1)} %cholesky.118), custom_call_target="Cholesky" | custom-call | tf_op jit(solution)/shard_map/jit(cholesky)/cholesky | solution.py:127
  515.3 10.0 %custom-call.15 = f32[1,128,128]{1,2,0:T(8,128)S(1)} custom-call(f32[1,128,128]{2,1,0:T(8,128)S(1)} %get-tuple-element.33), custom_call_target="InvertDiagBlocksLowerTriangular" | custom-call | tf_op jit(solution)/shard_map/jit(cholesky)/cholesky | solution.py:127
  525.8 11.7 %cholesky.105 = f32[128,128]{1,0:T(8,128)S(1)} custom-call(f32[128,128]{1,0:T(8,128)S(1)} %convolution_subtract_fusion.1), custom_call_target="Cholesky" | custom-call | tf_op jit(solution)/shard_map/jit(cholesky)/cholesky | solution.py:127
  539.7 4.1 while.1
  543.7 19.7 %custom-call.16 = f32[2,128,128]{1,2,0:T(8,128)S(1)} custom-call(f32[2,128,128]{2,1,0:T(8,128)S(1)} %get-tuple-element.10), custom_call_target="InvertDiagBlocksLowerTriangular" | custom-call | tf_op jit(solution)/shard_map/jit(_solve_triangular)/triangular_solve | solution.py:129
  566.3 4.8 concatenate.18
  571.1 11.7 %gather_fusion.3 = bf16[1024,2048]{1,0:T(8,128)(2,1)} fusion(bf16[1025,2048]{1,0:T(8,128)(2,1)} %concatenate.18, s32[1024]{0:T(1024)S(1)} %broadcast_clamp_fusion), kind=kCustom, calls=%fused_computation.3 | custom fusion | bytes 8392704 | tf_op jit(solution)/shard_map/gather | solution.py:90
  582.8 5.9 bitcast_reduce_fusion
  (81 shorter events, 24.6 us)
Async XLA Ops:
  7.2 245.4 %copy-start = (bf16[2,2048,384]{2,1,0:T(8,128)(2,1)S(1)}, bf16[2,2048,384]{2,1,0:T(8,128)(2,1)}, u32[]{:S(2)}) copy-start(bf16[2,2048,384]{2,1,0:T(8,128)(2,1)} %param.17) | copy-start | bytes 9437188
  36.4 100.6 %all-to-all-start = ((bf16[8,128,2048]{2,1,0:T(8,128)(2,1)}), bf16[8,128,2048]{2,1,0:T(8,128)(2,1)}, u32[]{:S(2)}, u32[]{:S(2)}) async-start(bf16[8,128,2048]{2,1,0:T(8,128)(2,1)} %fusion), calls=%async_computation | async-start | bytes 8388608 | tf_op jit(solution)/shard_map/all_to_all | solution.py:50
  137.0 5.2 copy-start.12
  137.0 109.9 %all-to-all-start.1 = ((bf16[8,128,2048]{2,1,0:T(8,128)(2,1)}), bf16[8,128,2048]{2,1,0:T(8,128)(2,1)}, u32[]{:S(2)}, u32[]{:S(2)}) async-start(bf16[8,128,2048]{2,1,0:T(8,128)(2,1)} %bitcast.178), calls=%async_computation.1 | async-start | bytes 8388608 | tf_op jit(solution)/shard_map/all_to_all | solution.py:49
  141.7 123.7 %all-gather.2.cloned.1.call-start = ((), (), s32[]{:S(2)}) async-start(), calls=%async_computation.3 | async-start | bytes 1179648 | tf_op jit(solution)/shard_map/all_gather | solution.py:43
  246.9 5.6 copy-start.13
  252.6 7.2 %copy-start.6 = (bf16[2,2048,384]{2,1,0:T(8,128)(2,1)S(1)}, bf16[2,2048,384]{2,1,0:T(8,128)(2,1)}, u32[]{:S(2)}) copy-start(bf16[2,2048,384]{2,1,0:T(8,128)(2,1)} %param.16) | copy-start | bytes 9437188
  258.9 0.9 copy-start.4
  265.4 6.6 %copy-start.8 = (bf16[8,2,64,384]{3,2,0,1:T(8,128)(2,1)S(1)}, bf16[8,2,64,384]{3,2,0,1:T(8,128)(2,1)}, u32[]{:S(2)}) copy-start(bf16[8,2,64,384]{3,2,0,1:T(8,128)(2,1)} %get-tuple-element.29) | copy-start | bytes 2359300
  265.4 8.0 %copy-start.2 = (f32[2,8,64,2048]{3,2,1,0:T(8,128)S(1)}, f32[2,8,64,2048]{3,2,1,0:T(8,128)}, u32[]{:S(2)}) copy-start(f32[2,8,64,2048]{3,2,1,0:T(8,128)} %fusion.14) | copy-start | bytes 25165828
  278.3 4.7 copy-start.14
  278.3 288.0 %all-to-all-start.2 = ((bf16[8,128,2048]{2,1,0:T(8,128)(2,1)}), bf16[8,128,2048]{2,1,0:T(8,128)(2,1)}, u32[]{:S(2)}, u32[]{:S(2)}) async-start(bf16[8,128,2048]{2,1,0:T(8,128)(2,1)} %bitcast.180), calls=%async_computation.2 | async-start | bytes 8388608 | tf_op jit(solution)/shard_map/all_to_all | solution.py:85
  283.0 63.4 %all-reduce.7.cloned.1.call-start = ((), (), s32[]{:S(2)}) async-start(), calls=%async_computation.4 | async-start | bytes 4718592 | tf_op jit(solution)/shard_map/psum | solution.py:103
  283.0 4.4 copy-start.10
  283.1 4.4 copy-start.11
  289.2 59.0 %copy-start.5 = (bf16[8,2,64,384]{3,2,0,1:T(8,128)(2,1)S(1)}, bf16[8,2,64,384]{3,2,0,1:T(8,128)(2,1)}, u32[]{:S(2)}) copy-start(bf16[8,2,64,384]{3,2,0,1:T(8,128)(2,1)} %copy-done.4) | copy-start | bytes 2359300
  289.2 208.4 %all-reduce.9.cloned.1.call-start = ((), (), s32[]{:S(2)}) async-start(), calls=%async_computation.5 | async-start | bytes 4194304 | tf_op jit(solution)/shard_map/psum | solution.py:120
  348.2 1.5 copy-start.7
  349.6 5.4 copy-start.9
  355.0 6.5 %copy-start.3 = (f32[2,3,384,256]{3,2,0,1:T(8,128)S(1)}, f32[2,3,384,256]{3,2,0,1:T(8,128)}, u32[]{:S(2)}) copy-start(f32[2,3,384,256]{3,2,0,1:T(8,128)} %all-reduce.7.cloned.1.call-done) | copy-start | bytes 7077892
  571.1 17.6 %copy-start.1 = (bf16[2,2048,384]{2,1,0:T(8,128)(2,1)S(1)}, bf16[2,2048,384]{2,1,0:T(8,128)(2,1)}, u32[]{:S(2)}) copy-start(bf16[2,2048,384]{2,1,0:T(8,128)(2,1)} %param.17) | copy-start | bytes 9437188
Sparse Core Ops, SparseCore 0:
  145.2 102.1 all-gather.1
  289.3 56.9 all-reduce.6
  361.6 135.9 all-reduce.8
where the time goes:
time: 600 us; the launch traced here: 595 us
  waiting for transfers between devices  370 us (62%)
  other arithmetic  69.8 us (12%)
  local copies, waits for them, and re-layouts  63 us (10%)
  matrix products  59.4 us (10%)
  starting transfers between devices  17.4 us (3%)
  between operations  15.7 us (3%)
    psum x1, waiting for transfers between devices, body(): power_sum = lax.psum(power, ('expert', 'replica'))  134 us
    all_to_all x1, waiting for transfers between devices, body(): lax.all_to_all(x_send, 'expert', split_axis=0, concat_axis=0, tiled=True)  97.3 us
    all_to_all x1, waiting for transfers between devices, body(): lax.all_to_all(dy_send, 'expert', split_axis=0, concat_axis=0, tiled=True)  81.4 us
    psum x1, waiting for transfers between devices, body(): projected_grads = lax.psum(partial_grads, 'replica')  56.9 us
    another operation x6, other arithmetic, body(): lower = jnp.linalg.cholesky(gram_total)  34.2 us
    another operation x3, other arithmetic, body(): jax.scipy.linalg.solve_triangular(lower, own_panel.T, lower=True)  19.7 us
  transfers between devices with their start and end apart: 6, of which 4 were waited for; matrix products, arithmetic and copies ran while one was open for 21% of the time, Pallas kernels for 0%

commit v1 on v0

--- a/solution.py
+++ b/solution.py
@@ -117,7 +117,7 @@
         "sjcd,sjcr->dr", dy_rows, down_mix, preferred_element_type=jnp.float32
     )
     panel_rows = model_width // group_count
-    power_sum = lax.psum(power, ("expert", "replica"))
+    power_sum = lax.psum(lax.psum(power, "expert"), "replica")
     gram_total = jnp.dot(
         power_sum.T, power_sum, precision=lax.Precision.HIGHEST, preferred_element_type=jnp.float32
     )

time: 600 us -> 632 us (1.053)
  waiting for transfers between devices: 370 us -> 392 us
  matrix products: 59.4 us -> 68.2 us
    psum x1 -> x2, waiting for transfers between devices: 134 us -> 185 us  [body(): power_sum = lax.psum(lax.psum(power, 'expert'), 'replica')]
    psum x1, waiting for transfers between devices: 56.9 us -> 28.8 us  [body(): projected_grads = lax.psum(partial_grads, 'replica')]
    dot_general x1, matrix products: 2.41 us -> 14.2 us  [body(): jnp.einsum('sjcf,jdf->sjcd', up_grad, up_weight, preferred_element_type=j...]
  transfers between devices with their start and end apart: 6 -> 7, of which waited for: 4 -> 5; matrix products, arithmetic and copies ran while one was open for 21% -> 21% of each run, Pallas kernels for 0% -> 0%
where the time goes in v1:
time: 632 us; the launch traced here: 627 us
  waiting for transfers between devices  392 us (62%)
  other arithmetic  71.4 us (11%)
  matrix products  68.2 us (11%)
  local copies, waits for them, and re-layouts  61.9 us (10%)
  starting transfers between devices  17.1 us (3%)
  between operations  15.7 us (2%)
    psum x2, waiting for transfers between devices, body(): power_sum = lax.psum(lax.psum(power, 'expert'), 'replica')  185 us
    all_to_all x1, waiting for transfers between devices, body(): lax.all_to_all(x_send, 'expert', split_axis=0, concat_axis=0, tiled=True)  97.4 us
    all_to_all x1, waiting for transfers between devices, body(): lax.all_to_all(dy_send, 'expert', split_axis=0, concat_axis=0, tiled=True)  81.4 us
    another operation x6, other arithmetic, body(): lower = jnp.linalg.cholesky(gram_total)  34.1 us
    psum x1, waiting for transfers between devices, body(): projected_grads = lax.psum(partial_grads, 'replica')  28.8 us
    another operation x3, other arithmetic, body(): jax.scipy.linalg.solve_triangular(lower, own_panel.T, lower=True)  19.7 us
    dot_general x1, matrix products, body(): jnp.einsum('sjcf,jdf->sjcd', up_grad, up_weight, preferred_element_type=j...  14.2 us
  transfers between devices with their start and end apart: 7, of which 5 were waited for; matrix products, arithmetic and copies ran while one was open for 21% of the time, Pallas kernels for 0%

profile of v1, /device:TPU:0, one launch (start us, length us, event | category | flops | bytes accessed | tf_op | source)
XLA Modules:
  0.0 626.8 jit_solution(7083593260471382092)
XLA Ops:
  8.3 4.3 scatter_custom_fusion
  15.4 9.9 %gather_fusion = bf16[1024,2048]{1,0:T(8,128)(2,1)} fusion(bf16[129,2048]{1,0:T(8,128)(2,1)} %concatenate.15, s32[1024]{0:T(1024)S(1)} %get-tuple-element.37), kind=kCustom, calls=%fused_computation | custom fusion | bytes 8392704 | tf_op jit(solution)/shard_map/gather | solution.py:39
  25.4 6.1 gather_fusion.1
  31.5 4.9 fusion
  36.4 7.3 %all-to-all-start = ((bf16[8,128,2048]{2,1,0:T(8,128)(2,1)}), bf16[8,128,2048]{2,1,0:T(8,128)(2,1)}, u32[]{:S(2)}, u32[]{:S(2)}) async-start(bf16[8,128,2048]{2,1,0:T(8,128)(2,1)} %fusion), calls=%async_computation | async-start | bytes 8388608 | tf_op jit(solution)/shard_map/all_to_all | solution.py:50
  45.6 9.9 %gather_fusion.2 = bf16[1024,2048]{1,0:T(8,128)(2,1)} fusion(bf16[129,2048]{1,0:T(8,128)(2,1)} %concatenate.17, s32[1024]{0:T(1024)S(1)} %get-tuple-element.37), kind=kCustom, calls=%fused_computation.2 | custom fusion | bytes 8392704 | tf_op jit(solution)/shard_map/gather | solution.py:38
  55.5 81.4 %all-to-all-done = bf16[8,128,2048]{2,1,0:T(8,128)(2,1)} async-done(((bf16[8,128,2048]{2,1,0:T(8,128)(2,1)}), bf16[8,128,2048]{2,1,0:T(8,128)(2,1)}, u32[]{:S(2)}, u32[]{:S(2)}) %all-to-all-start) | async-done | bytes 4194336 | tf_op jit(solution)/shard_map/all_to_all | solution.py:50
  137.0 4.7 all-to-all-start.1
  142.9 6.6 %fusion.12 = f32[2,8,64,384]{3,2,1,0:T(8,128)} fusion(bf16[8,2,64,2048]{3,2,1,0:T(8,128)(2,1)} %bitcast.3, bf16[2,384,2048]{2,1,0:T(8,128)(2,1)} %param.18), kind=kOutput, calls=%fused_computation.22 | convolution fusion | flops 1610612736 | bytes 8912896 | tf_op jit(solution)/shard_map/sjcd,jfd->sjcf/dot_general | solution.py:71
  149.5 97.4 %all-to-all-done.1 = bf16[8,128,2048]{2,1,0:T(8,128)(2,1)} async-done(((bf16[8,128,2048]{2,1,0:T(8,128)(2,1)}), bf16[8,128,2048]{2,1,0:T(8,128)(2,1)}, u32[]{:S(2)}, u32[]{:S(2)}) %all-to-all-start.1) | async-done | bytes 4194336 | tf_op jit(solution)/shard_map/all_to_all | solution.py:49
  246.9 5.6 fusion.4
  252.5 6.4 %fusion.36 = (bf16[8,2,64,384]{3,2,0,1:T(8,128)(2,1)}, bf16[8,2,64,384]{3,2,0,1:T(8,128)(2,1)}, bf16[8,2,64,384]{3,2,0,1:T(8,128)(2,1)}) fusion(f32[2,8,64,384]{3,2,1,0:T(8,128)S(1)} %fusion.4, f32[2,8,64,384]{3,2,1,0:T(8,128)S(1)} %copy-done.8, bf16[2,2048,384]{2,1,0:T(8,128)(2,1)S(1)} %copy-done, bf16[8,2,64,2048]{3,2,1,0:T(8,128)(2,1)} %bitcast.8), kind=kOutput, calls=%fused_computation.47 | convolution fusion | flops 1616510976 | bytes 12845056 | tf_op jit(solution)/shard_map/sjcd,jdf->sjcf/dot_general | solution.py:54
  258.9 3.9 convolution_convert_fusion.1
  265.5 5.5 convolution_bitcast_fusion
  270.9 3.3 pad_maximum_fusion
  274.3 4.6 fusion.14
  278.8 14.2 %fusion.1 = bf16[8,2,64,2048]{3,2,0,1:T(8,128)(2,1)S(1)} fusion(f32[2,8,64,2048]{3,2,1,0:T(8,128)S(1)} %fusion.14, bf16[8,2,64,384]{3,2,0,1:T(8,128)(2,1)S(1)} %copy-done.6, bf16[2,2048,384]{2,1,0:T(8,128)(2,1)S(1)} %copy-done), kind=kOutput, calls=%fused_computation.11 | convolution fusion | flops 1614807040 | bytes 16515072 | tf_op jit(solution)/shard_map/sjcf,jdf->sjcd/dot_general | solution.py:79
  295.5 4.6 all-to-all-start.2
  300.2 28.8 %all-reduce.8.cloned.1.call-done = f32[2,3,384,256]{3,2,0,1:T(8,128)} async-done(((f32[2,3,384,256]{3,2,0,1:T(8,128)}), f32[2,3,384,256]{3,2,0,1:T(8,128)}) %all-reduce.8.cloned.1.call-update) | async-done | bytes 2359312 | tf_op jit(solution)/shard_map/psum | solution.py:103
  330.8 5.2 fusion.20
  336.5 6.1 fusion.26
  342.6 133.6 %all-reduce.10.cloned.1.call-done = f32[2048,256]{1,0:T(8,128)} async-done(((f32[2048,256]{1,0:T(8,128)}), f32[2048,256]{1,0:T(8,128)}) %all-reduce.10.cloned.1.call-update) | async-done | bytes 2097168 | tf_op jit(solution)/shard_map/psum | solution.py:120
  478.0 51.2 %all-reduce.12.cloned.1.call-done = f32[2048,256]{1,0:T(8,128)} async-done(((f32[2048,256]{1,0:T(8,128)}), f32[2048,256]{1,0:T(8,128)}) %all-reduce.12.cloned.1.call-update) | async-done | bytes 2097168 | tf_op jit(solution)/shard_map/psum | solution.py:120
  529.1 5.7 fusion.72
  535.0 11.7 %cholesky.50 = f32[128,128]{1,0:T(8,128)S(1)} custom-call(f32[128,128]{1,0:T(8,128)S(1)} %cholesky.118), custom_call_target="Cholesky" | custom-call | tf_op jit(solution)/shard_map/jit(cholesky)/cholesky | solution.py:127
  546.8 9.8 %custom-call.15 = f32[1,128,128]{1,2,0:T(8,128)S(1)} custom-call(f32[1,128,128]{2,1,0:T(8,128)S(1)} %get-tuple-element.33), custom_call_target="InvertDiagBlocksLowerTriangular" | custom-call | tf_op jit(solution)/shard_map/jit(cholesky)/cholesky | solution.py:127
  557.1 11.8 %cholesky.105 = f32[128,128]{1,0:T(8,128)S(1)} custom-call(f32[128,128]{1,0:T(8,128)S(1)} %convolution_subtract_fusion.1), custom_call_target="Cholesky" | custom-call | tf_op jit(solution)/shard_map/jit(cholesky)/cholesky | solution.py:127
  571.1 4.0 while.1
  575.2 19.7 %custom-call.16 = f32[2,128,128]{1,2,0:T(8,128)S(1)} custom-call(f32[2,128,128]{2,1,0:T(8,128)S(1)} %get-tuple-element.10), custom_call_target="InvertDiagBlocksLowerTriangular" | custom-call | tf_op jit(solution)/shard_map/jit(_solve_triangular)/triangular_solve | solution.py:129
  597.7 4.7 concatenate.18
  602.5 11.7 %gather_fusion.3 = bf16[1024,2048]{1,0:T(8,128)(2,1)} fusion(bf16[1025,2048]{1,0:T(8,128)(2,1)} %concatenate.18, s32[1024]{0:T(1024)S(1)} %broadcast_clamp_fusion), kind=kCustom, calls=%fused_computation.3 | custom fusion | bytes 8392704 | tf_op jit(solution)/shard_map/gather | solution.py:90
  614.2 5.9 bitcast_reduce_fusion
  (74 shorter events, 24.5 us)
Async XLA Ops:
  7.2 245.4 %copy-start = (bf16[2,2048,384]{2,1,0:T(8,128)(2,1)S(1)}, bf16[2,2048,384]{2,1,0:T(8,128)(2,1)}, u32[]{:S(2)}) copy-start(bf16[2,2048,384]{2,1,0:T(8,128)(2,1)} %param.17) | copy-start | bytes 9437188
  36.4 100.6 %all-to-all-start = ((bf16[8,128,2048]{2,1,0:T(8,128)(2,1)}), bf16[8,128,2048]{2,1,0:T(8,128)(2,1)}, u32[]{:S(2)}, u32[]{:S(2)}) async-start(bf16[8,128,2048]{2,1,0:T(8,128)(2,1)} %fusion), calls=%async_computation | async-start | bytes 8388608 | tf_op jit(solution)/shard_map/all_to_all | solution.py:50
  137.0 4.7 copy-start.7
  137.0 109.9 %all-to-all-start.1 = ((bf16[8,128,2048]{2,1,0:T(8,128)(2,1)}), bf16[8,128,2048]{2,1,0:T(8,128)(2,1)}, u32[]{:S(2)}, u32[]{:S(2)}) async-start(bf16[8,128,2048]{2,1,0:T(8,128)(2,1)} %bitcast.178), calls=%async_computation.1 | async-start | bytes 8388608 | tf_op jit(solution)/shard_map/all_to_all | solution.py:49
  141.7 117.2 %all-gather.2.cloned.1.call-start = ((), (), s32[]{:S(2)}) async-start(), calls=%async_computation.3 | async-start | bytes 1179648 | tf_op jit(solution)/shard_map/all_gather | solution.py:43
  142.4 186.6 %all-reduce.8.cloned.1.call-start = ((), (), s32[]{:S(2)}) async-start(), calls=%async_computation.4 | async-start | bytes 4718592 | tf_op jit(solution)/shard_map/psum | solution.py:103
  246.9 5.6 copy-start.8
  258.9 3.9 copy-start.5
  258.9 5.2 copy-start.3
  274.2 4.6 copy-start.6
  295.5 302.2 %all-to-all-start.2 = ((bf16[8,128,2048]{2,1,0:T(8,128)(2,1)}), bf16[8,128,2048]{2,1,0:T(8,128)(2,1)}, u32[]{:S(2)}, u32[]{:S(2)}) async-start(bf16[8,128,2048]{2,1,0:T(8,128)(2,1)} %bitcast.180), calls=%async_computation.2 | async-start | bytes 8388608 | tf_op jit(solution)/shard_map/all_to_all | solution.py:85
  300.1 30.7 %copy-start.9 = (bf16[8,2,64,384]{3,2,0,1:T(8,128)(2,1)S(1)}, bf16[8,2,64,384]{3,2,0,1:T(8,128)(2,1)}, u32[]{:S(2)}) copy-start(bf16[8,2,64,384]{3,2,0,1:T(8,128)(2,1)} %get-tuple-element.27) | copy-start | bytes 2359300
  300.1 176.1 %all-reduce.10.cloned.1.call-start = ((), (), s32[]{:S(2)}) async-start(), calls=%async_computation.5 | async-start | bytes 4194304 | tf_op jit(solution)/shard_map/psum | solution.py:120
  330.8 5.2 copy-start.4
  342.5 133.7 %copy-start.2 = (f32[2,3,384,256]{3,2,0,1:T(8,128)S(1)}, f32[2,3,384,256]{3,2,0,1:T(8,128)}, u32[]{:S(2)}) copy-start(f32[2,3,384,256]{3,2,0,1:T(8,128)} %all-reduce.8.cloned.1.call-done) | copy-start | bytes 7077892
  342.6 186.5 %all-reduce.12.cloned.1.call-start = ((), (), s32[]{:S(2)}) async-start(), calls=%async_computation.6 | async-start | bytes 4194304 | tf_op jit(solution)/shard_map/psum | solution.py:120
  602.5 17.6 %copy-start.1 = (bf16[2,2048,384]{2,1,0:T(8,128)(2,1)S(1)}, bf16[2,2048,384]{2,1,0:T(8,128)(2,1)}, u32[]{:S(2)}) copy-start(bf16[2,2048,384]{2,1,0:T(8,128)(2,1)} %param.17) | copy-start | bytes 9437188
Sparse Core Ops, SparseCore 0:
  145.2 102.2 all-gather.1
  274.4 54.6 all-reduce.7
  342.7 133.4 all-reduce.9
  478.4 50.6 all-reduce.11
